TPU v7x, 512 devices: a whole 4x4x16 slice. The times are simulated.
512 devices in a mesh: tm: 8 (over x, core), pair: 64 (over z, y).
Axes of the slice: x: 4, y: 4, z: 16, core: 2. Of those that a mesh axis runs over, the one named last changes fastest.
Arguments:
- traces: float32 [16, 8192, 1024], P('tm', 'pair'), may hold values from -6 to 6
- owner: int32 [64], replicated, may hold values from 0 to 63, each once
- tiles: int32 [192, 2], P('pair'), may hold values from 0 to 63, as said below
- counts: int32 [64], P('pair'), may hold values from 1 to 3, as said below
Outputs:
- stacks: float32 [192, 128, 16384], P('pair', None, 'tm')
Inputs may be any that keep to these rules, and one draw needn't show every extreme that they name: `tiles`: each row names fiber blocks a <= b with b - a at most 6. `counts`: the first that many of an index's 3 slots are live; some index has all 3 live.
All inputs are finite; a program needn't handle non-finite values.
Results may differ from a plain program's by a relative error of at most 0.0038.
Values may be sent and summed in bfloat16 or wider, within the bound.
A program may use at most 64 MiB of HBM per device.

v0:
```python
import math
import jax
import jax.numpy as jnp
from jax import lax
from jax.sharding import PartitionSpec as P

NT = 1024
NF = 128
LOW_BIN = 8
LAGS = 128


def forward_table():
    samples = jnp.arange(NT, dtype=jnp.int32)
    bins = LOW_BIN + jnp.arange(NF, dtype=jnp.int32)
    phase = samples[:, None] * bins[None, :] % NT
    angle = phase.astype(jnp.float32) * (2.0 * math.pi / NT)
    return jnp.concatenate([jnp.cos(angle), -jnp.sin(angle)], axis=1)


def inverse_table():
    shifts = jnp.arange(LAGS, dtype=jnp.int32) - LAGS // 2
    bins = LOW_BIN + jnp.arange(NF, dtype=jnp.int32)
    phase = jnp.mod(shifts[:, None] * bins[None, :], NT)
    angle = phase.astype(jnp.float32) * (2.0 * math.pi / NT)
    return (jnp.cos(angle), -jnp.sin(angle))


def window_sum(values):
    widths = [(0, 0)] * (values.ndim - 1) + [(2, 2)]
    padded = jnp.pad(values, widths)
    total = padded[..., 0:NF]
    for offset in range(1, 5):
        total = total + padded[..., offset : offset + NF]
    return total


def whiten(spectrum):
    real_part = spectrum[..., :NF]
    imag_part = spectrum[..., NF:]
    power = real_part * real_part + imag_part * imag_part
    counted = window_sum(jnp.ones((NF,), jnp.float32))
    smooth = window_sum(power) / counted
    level = jnp.mean(power, axis=-1, keepdims=True)
    factor = lax.rsqrt(smooth + 0.05 * level + 1e-06)
    return jnp.concatenate([real_part * factor, imag_part * factor], axis=-1).astype(jnp.bfloat16)


def lookup(owner, fiber_ids):
    onehot = fiber_ids[..., None] == jnp.arange(owner.shape[0], dtype=jnp.int32)
    return jnp.sum(jnp.where(onehot, owner, 0), axis=-1)


def shards(traces, owner, tiles, counts):
    seg_count, block, samples = traces.shape
    rows = seg_count * block
    width = 2 * NF
    spectrum = jnp.dot(
        traces.reshape(rows, samples), forward_table(), precision=lax.Precision.HIGHEST
    )
    white = whiten(spectrum)
    time_count = lax.axis_size("tm")
    segments = seg_count * time_count
    share = block // time_count
    slots = tiles.shape[0]
    scale = 1.0 / math.sqrt(segments * NF)
    cos_part, sin_part = inverse_table()
    every = lax.all_gather(white[None], "pair", axis=0, tiled=True)
    stored = lookup(owner, tiles)
    picked = jnp.take(every, stored.reshape(-1), axis=0).reshape(slots, 2, rows, width)
    number = picked.shape[0]
    left = picked[:, 0].reshape(number, seg_count, block, width)
    right = picked[:, 1].reshape(number, seg_count, block, width)
    left_all = lax.all_to_all(left, "tm", split_axis=2, concat_axis=1, tiled=True)
    right_all = lax.all_gather(right, "tm", axis=1, tiled=True)
    left_real = left_all[..., :NF]
    left_imag = left_all[..., NF:]
    right_real = right_all[..., :NF]
    right_imag = right_all[..., NF:]
    cross_real = jnp.einsum(
        "qsif,qsjf->qfij", left_real, right_real, preferred_element_type=jnp.float32
    )
    cross_real = cross_real + jnp.einsum(
        "qsif,qsjf->qfij", left_imag, right_imag, preferred_element_type=jnp.float32
    )
    cross_imag = jnp.einsum(
        "qsif,qsjf->qfij", left_real, right_imag, preferred_element_type=jnp.float32
    )
    cross_imag = cross_imag - jnp.einsum(
        "qsif,qsjf->qfij", left_imag, right_real, preferred_element_type=jnp.float32
    )
    cross_real = cross_real.reshape(number, NF, share * block)
    cross_imag = cross_imag.reshape(number, NF, share * block)
    lagged = jnp.einsum("lf,qfx->qlx", cos_part, cross_real, precision=lax.Precision.HIGHEST)
    lagged = lagged + jnp.einsum(
        "lf,qfx->qlx", sin_part, cross_imag, precision=lax.Precision.HIGHEST
    )
    partial_value = lagged * scale
    live = (jnp.arange(slots, dtype=jnp.int32) < counts[0]).astype(jnp.float32)
    return partial_value * live[:, None, None]


def solution(mesh):
    placed = (P("tm", "pair", None), P(), P("pair", None), P("pair"))
    return jax.shard_map(
        shards, mesh=mesh, in_specs=placed, out_specs=P("pair", None, "tm"), check_vma=False
    )
```

profile of v0, /device:TPU:1, one launch (start us, length us, event | category | flops | bytes accessed | tf_op | source)
XLA Modules:
  0.0 259.8 jit_solution(12651376614939929892)
XLA Ops:
  6.6 2.1 fusion.9
  8.6 1.8 convolution_bitcast_fusion
  10.5 0.1 fusion.27
  10.6 0.1 fusion.13
  10.8 0.8 copy.56
  11.6 0.1 copy.55
  11.7 0.2 fusion.23
  11.9 0.1 reshape.100
  12.0 154.2 %all-gather.3.cloned.1.call-done = bf16[64,256,256]{2,1,0:T(8,128)(2,1)} async-done(((bf16[1,256,256]{2,1,0:T(8,128)(2,1)}), bf16[64,256,256]{2,1,0:T(8,128)(2,1)}) %all-gather.3.cloned.1.call-update) | async-done | bytes 8388624 | tf_op jit(solution)/shard_map/all_gather | solution.py:68
  166.3 4.0 %gather_fusion = bf16[6,256,256]{2,1,0:T(8,128)(2,1)S(1)} fusion(bf16[64,256,256]{2,1,0:T(8,128)(2,1)} %all-gather.3.cloned.1.call-done, s32[1024]{0:T(1024)S(1)} %pad_clamp_fusion), kind=kCustom, calls=%fused_computation | custom fusion | bytes 1572888 | tf_op jit(solution)/shard_map/jit(_take)/gather | solution.py:70
  170.2 0.1 broadcast_select_fusion
  170.4 0.1 fusion.40
  170.5 0.8 copy.61
  171.3 1.2 copy.57
  172.4 12.6 %all-to-all-start = ((bf16[3,2,128,256]{3,1,0,2:T(2,128)(2,1)}), bf16[3,2,128,256]{3,1,0,2:T(2,128)(2,1)S(1)}, u32[]{:S(2)}, u32[]{:S(2)}) async-start(bf16[3,2,128,256]{3,1,0,2:T(2,128)(2,1)} %copy.57), calls=%async_computation | async-start | bytes 786432 | tf_op jit(solution)/shard_map/all_to_all | solution.py:74
  185.6 7.4 %all-to-all-done = bf16[3,2,128,256]{3,1,0,2:T(2,128)(2,1)S(1)} async-done(((bf16[3,2,128,256]{3,1,0,2:T(2,128)(2,1)}), bf16[3,2,128,256]{3,1,0,2:T(2,128)(2,1)S(1)}, u32[]{:S(2)}, u32[]{:S(2)}) %all-to-all-start) | async-done | bytes 393248 | tf_op jit(solution)/shard_map/all_to_all | solution.py:74
  193.1 0.1 fusion.41
  193.2 1.7 copy.72
  194.9 1.1 copy.74
  196.0 13.7 %all-gather.5.cloned.1.call-done = bf16[3,16,128,256]{3,2,0,1:T(8,128)(2,1)} async-done(((bf16[3,2,128,256]{3,2,0,1:T(8,128)(2,1)}), bf16[3,16,128,256]{3,2,0,1:T(8,128)(2,1)}) %all-gather.5.cloned.1.call-update) | async-done | bytes 3145744 | tf_op jit(solution)/shard_map/all_gather | solution.py:75
  209.8 4.0 %fusion.39 = (bf16[3,16,128,128]{3,2,0,1:T(8,128)(2,1)}, bf16[3,16,128,128]{3,2,0,1:T(8,128)(2,1)}) fusion(bf16[3,16,128,256]{3,2,0,1:T(8,128)(2,1)} %all-gather.5.cloned.1.call-done), kind=kLoop, calls=%fused_computation.71 | loop fusion | bytes 6291456 | tf_op jit(solution)/shard_map/slice | solution.py:79
  213.7 2.8 %copy.75 = bf16[3,16,128,128]{2,1,3,0:T(8,128)(2,1)} copy(bf16[3,16,128,128]{3,2,0,1:T(8,128)(2,1)} %get-tuple-element.9) | data formatting | bytes 3145728
  216.5 2.8 %copy.73 = bf16[3,16,128,128]{2,1,3,0:T(8,128)(2,1)} copy(bf16[3,16,128,128]{3,2,0,1:T(8,128)(2,1)} %get-tuple-element.10) | data formatting | bytes 3145728
  219.3 3.0 %fusion.43 = f32[3,128,16,128]{3,2,1,0:T(8,128)S(1)} fusion(bf16[3,16,16,128]{1,2,3,0:T(8,128)(2,1)} %copy.72, bf16[3,16,128,128]{2,1,3,0:T(8,128)(2,1)} %copy.75), kind=kOutput, calls=%fused_computation.75 | convolution fusion | flops 25165824 | bytes 4915200 | tf_op jit(solution)/shard_map/qsif,qsjf->qfij/dot_general | solution.py:86
  222.3 2.6 %fusion.42 = f32[3,128,16,128]{3,2,1,0:T(8,128)} fusion(bf16[3,16,16,128]{1,2,3,0:T(8,128)(2,1)S(1)} %copy-done.1, bf16[3,16,128,128]{2,1,3,0:T(8,128)(2,1)S(1)} %copy-done.2), kind=kOutput, calls=%fused_computation.74 | convolution fusion | flops 25165824 | bytes 4915200 | tf_op jit(solution)/shard_map/qsif,qsjf->qfij/dot_general | solution.py:80
  225.0 2.6 %convolution_subtract_fusion = f32[3,128,16,128]{3,2,1,0:T(8,128)} fusion(f32[3,128,16,128]{3,2,1,0:T(8,128)S(1)} %fusion.43, bf16[3,16,16,128]{1,2,3,0:T(8,128)(2,1)S(1)} %copy.74, bf16[3,16,128,128]{2,1,3,0:T(8,128)(2,1)S(1)} %copy-done.2), kind=kOutput, calls=%fused_computation.2 | convolution fusion | flops 25952256 | bytes 8060928 | tf_op jit(solution)/shard_map/qsif,qsjf->qfij/dot_general | solution.py:89
  227.6 3.5 %copy.71 = f32[3,128,16,128]{1,3,2,0:T(8,128)} copy(f32[3,128,16,128]{3,2,1,0:T(8,128)} %convolution_subtract_fusion) | data formatting | bytes 6291456 | tf_op jit(solution)/shard_map/reshape | solution.py:93
  231.1 5.0 %convolution_add_fusion = f32[3,128,16,128]{3,2,1,0:T(8,128)} fusion(f32[3,128,16,128]{3,2,1,0:T(8,128)} %fusion.42, bf16[3,16,16,128]{1,2,3,0:T(8,128)(2,1)S(1)} %copy.74, bf16[3,16,128,128]{2,1,3,0:T(8,128)(2,1)} %copy.75), kind=kOutput, calls=%fused_computation.3 | convolution fusion | flops 25952256 | bytes 8060928 | tf_op jit(solution)/shard_map/qsif,qsjf->qfij/dot_general | solution.py:83
  236.1 3.6 %copy.70 = f32[3,128,16,128]{1,3,2,0:T(8,128)} copy(f32[3,128,16,128]{3,2,1,0:T(8,128)} %convolution_add_fusion) | data formatting | bytes 6291456 | tf_op jit(solution)/shard_map/reshape | solution.py:92
  239.7 5.0 %fusion.16 = f32[3,2048,128]{2,1,0:T(8,128)S(1)} fusion(f32[3,128,2048]{1,2,0:T(8,128)} %bitcast.41, s32[128]{0:T(128)S(1)} %get-tuple-element.18, s32[128]{0:T(128)S(1)} %get-tuple-element.17), kind=kOutput, calls=%fused_computation.37 | convolution fusion | flops 1208188928 | bytes 6292480 | tf_op jit(solution)/shard_map/lf,qfx->qlx/dot_general | solution.py:94
  244.7 4.7 %multiply_bitcast_fusion = f32[3,128,2048]{1,2,0:T(8,128)} fusion(f32[3,2048,128]{2,1,0:T(8,128)S(1)} %fusion.16, f32[3,128,2048]{1,2,0:T(8,128)S(1)} %bitcast.40, f32[3]{0:T(128)S(1)} %compare_select_fusion.3, s32[128]{0:T(128)S(1)} %get-tuple-element.18, s32[128]{0:T(128)S(1)} %get-tuple-element.17), kind=kOutput, calls=%fused_computation.1 | convolution fusion | flops 1209778176 | bytes 9438220 | tf_op jit(solution)/shard_map/lf,qfx->qlx/dot_general | solution.py:95
  249.4 3.5 %copy.67 = f32[3,128,2048]{2,1,0:T(8,128)} copy(f32[3,128,2048]{1,2,0:T(8,128)} %multiply_bitcast_fusion) | data formatting | bytes 6291456 | tf_op jit(solution)/shard_map/mul | solution.py:100
  (28 shorter events, 0.3 us)
Async XLA Ops:
  6.5 2.1 copy-start
  6.5 5.1 %copy-start.4 = (s32[3,2]{0,1:T(2,128)S(1)}, s32[3,2]{0,1:T(2,128)}, u32[]{:S(2)}) copy-start(s32[3,2]{0,1:T(2,128)} %param.6) | copy-start | bytes 76
  6.5 5.2 %copy-start.5 = (s32[64]{0:T(128)S(1)}, s32[64]{0:T(128)}, u32[]{:S(2)}) copy-start(s32[64]{0:T(128)} %param.5) | copy-start | bytes 772
  6.5 159.7 %all-gather.3.cloned.1.call-start = ((), (), s32[]{:S(2)}) async-start(), calls=%async_computation.1 | async-start | bytes 8519680 | tf_op jit(solution)/shard_map/all_gather | solution.py:68
  11.6 198.2 %all-gather.5.cloned.1.call-start = ((), (), s32[]{:S(2)}) async-start(), calls=%async_computation.2 | async-start | bytes 3538944 | tf_op jit(solution)/shard_map/all_gather | solution.py:75
  172.4 20.6 %all-to-all-start = ((bf16[3,2,128,256]{3,1,0,2:T(2,128)(2,1)}), bf16[3,2,128,256]{3,1,0,2:T(2,128)(2,1)S(1)}, u32[]{:S(2)}, u32[]{:S(2)}) async-start(bf16[3,2,128,256]{3,1,0,2:T(2,128)(2,1)} %copy.57), calls=%async_computation | async-start | bytes 786432 | tf_op jit(solution)/shard_map/all_to_all | solution.py:74
  219.3 3.0 %copy-start.1 = (bf16[3,16,16,128]{1,2,3,0:T(8,128)(2,1)S(1)}, bf16[3,16,16,128]{1,2,3,0:T(8,128)(2,1)}, u32[]{:S(2)}) copy-start(bf16[3,16,16,128]{1,2,3,0:T(8,128)(2,1)} %copy.72) | copy-start | bytes 589828
  219.3 3.0 %copy-start.2 = (bf16[3,16,128,128]{2,1,3,0:T(8,128)(2,1)S(1)}, bf16[3,16,128,128]{2,1,3,0:T(8,128)(2,1)}, u32[]{:S(2)}) copy-start(bf16[3,16,128,128]{2,1,3,0:T(8,128)(2,1)} %copy.73) | copy-start | bytes 4718596
  239.7 5.0 %copy-start.3 = (f32[3,128,16,128]{1,3,2,0:T(8,128)S(1)}, f32[3,128,16,128]{1,3,2,0:T(8,128)}, u32[]{:S(2)}) copy-start(f32[3,128,16,128]{1,3,2,0:T(8,128)} %copy.71) | copy-start | bytes 9437188
Sparse Core Ops, SparseCore 0:
  11.7 154.5 all-gather.2
  171.4 38.3 all-gather.4
where the time goes:
time: 260 us
  waiting for transfers between devices  175 us (67%)
  local copies, waits for them, and re-layouts  30.1 us (12%)
  matrix products  24.7 us (10%)
  between operations  14.2 us (5%)
  starting transfers between devices  12.6 us (5%)
  other arithmetic  2.73 us (1%)
    all_gather x1, waiting for transfers between devices, shards(): every = lax.all_gather(white[None], 'pair', axis=0, tiled=True)  154 us
    all_gather x1, waiting for transfers between devices, shards(): right_all = lax.all_gather(right, 'tm', axis=1, tiled=True)  13.7 us
    all_to_all x1, starting transfers between devices, shards(): lax.all_to_all(left, 'tm', split_axis=2, concat_axis=1, tiled=True)  12.6 us
    unnamed x17, local copies, waits for them, and re-layouts  8.55 us
    all_to_all x1, waiting for transfers between devices, shards(): lax.all_to_all(left, 'tm', split_axis=2, concat_axis=1, tiled=True)  7.41 us
  transfers between devices with their start and end apart: 3, of which 3 were waited for; matrix products, arithmetic and copies ran while one was open for 2% of the time, Pallas kernels for 0%

commit v1 on v0

--- a/solution.py
+++ b/solution.py
@@ -8,6 +8,11 @@
 NF = 128
 LOW_BIN = 8
 LAGS = 128
+
+
+def exchange_gather(x, axis, dim):
+    repeated = jnp.stack([x] * lax.axis_size(axis))
+    return jnp.concatenate(lax.all_to_all(repeated, axis, 0, 0), axis=dim)
 
 
 def forward_table():
@@ -72,7 +77,7 @@
     left = picked[:, 0].reshape(number, seg_count, block, width)
     right = picked[:, 1].reshape(number, seg_count, block, width)
     left_all = lax.all_to_all(left, "tm", split_axis=2, concat_axis=1, tiled=True)
-    right_all = lax.all_gather(right, "tm", axis=1, tiled=True)
+    right_all = exchange_gather(right, "tm", 1)
     left_real = left_all[..., :NF]
     left_imag = left_all[..., NF:]
     right_real = right_all[..., :NF]

time: 260 us -> 282 us (1.085)
  waiting for transfers between devices: 175 us -> 196 us
  starting transfers between devices: 12.6 us -> 17.8 us
    all_to_all x0 -> x1, waiting for transfers between devices: none -> 34 us  [exchange_gather(): return jnp.concatenate(lax.all_to_all(repeated, axis, 0, 0), axis=dim)]
    all_gather x1 -> x0, waiting for transfers between devices: 13.7 us -> none  [shards(): right_all = lax.all_gather(right, 'tm', axis=1, tiled=True)]
    unnamed x17 -> x15, local copies, waits for them, and re-layouts: 8.55 us -> 3.01 us
    all_to_all x0 -> x1, starting transfers between devices: none -> 5.19 us  [exchange_gather(): return jnp.concatenate(lax.all_to_all(repeated, axis, 0, 0), axis=dim)]
    reshape x0 -> x1, local copies, waits for them, and re-layouts: none -> 4.17 us  [exchange_gather(): return jnp.concatenate(lax.all_to_all(repeated, axis, 0, 0), axis=dim)]
    another operation x1 -> x2, local copies, waits for them, and re-layouts: 0.77 us -> 4.8 us  [exchange_gather(): repeated = jnp.stack([x] * lax.axis_size(axis))]
    slice x1 -> x0, local copies, waits for them, and re-layouts: 3.95 us -> none  [shards(): right_imag = right_all[..., NF:]]
  transfers between devices with their start and end apart: 3 -> 3, of which waited for: 3 -> 3; matrix products, arithmetic and copies ran while one was open for 2% -> 1% of each run, Pallas kernels for 0% -> 0%
where the time goes in v1:
time: 282 us
  waiting for transfers between devices  196 us (70%)
  local copies, waits for them, and re-layouts  28.8 us (10%)
  matrix products  22.7 us (8%)
  starting transfers between devices  17.8 us (6%)
  between operations  14.2 us (5%)
    all_gather x1, waiting for transfers between devices, shards(): every = lax.all_gather(white[None], 'pair', axis=0, tiled=True)  154 us
    all_to_all x1, waiting for transfers between devices, exchange_gather(): return jnp.concatenate(lax.all_to_all(repeated, axis, 0, 0), axis=dim)  34 us
    all_to_all x1, starting transfers between devices, shards(): lax.all_to_all(left, 'tm', split_axis=2, concat_axis=1, tiled=True)  12.6 us
    all_to_all x1, waiting for transfers between devices, shards(): lax.all_to_all(left, 'tm', split_axis=2, concat_axis=1, tiled=True)  7.63 us
  transfers between devices with their start and end apart: 3, of which 3 were waited for; matrix products, arithmetic and copies ran while one was open for 1% of the time, Pallas kernels for 0%

profile of v1, /device:TPU:1, one launch (start us, length us, event | category | flops | bytes accessed | tf_op | source)
XLA Modules:
  0.0 282.1 jit_solution(18360366062789378446)
XLA Ops:
  6.6 2.1 fusion.15
  8.6 1.8 convolution_bitcast_fusion
  10.5 0.1 fusion.33
  10.6 0.1 fusion.19
  10.8 0.8 copy.54
  11.6 0.1 copy.53
  11.7 0.2 fusion.29
  11.9 0.1 reshape.108
  12.0 154.3 %all-gather.2.cloned.1.call-done = bf16[64,256,256]{2,1,0:T(8,128)(2,1)} async-done(((bf16[1,256,256]{2,1,0:T(8,128)(2,1)}), bf16[64,256,256]{2,1,0:T(8,128)(2,1)}) %all-gather.2.cloned.1.call-update) | async-done | bytes 8388624 | tf_op jit(solution)/shard_map/all_gather | solution.py:73
  166.3 4.0 %gather_fusion = bf16[6,256,256]{2,1,0:T(8,128)(2,1)S(1)} fusion(bf16[64,256,256]{2,1,0:T(8,128)(2,1)} %all-gather.2.cloned.1.call-done, s32[1024]{0:T(1024)S(1)} %pad_clamp_fusion), kind=kCustom, calls=%fused_computation | custom fusion | bytes 1572888 | tf_op jit(solution)/shard_map/jit(_take)/gather | solution.py:75
  170.2 0.1 broadcast_select_fusion
  170.4 0.1 fusion.45
  170.5 1.2 copy.55
  171.6 12.6 %all-to-all-start = ((bf16[3,2,128,256]{3,1,0,2:T(2,128)(2,1)}), bf16[3,2,128,256]{3,1,0,2:T(2,128)(2,1)S(1)}, u32[]{:S(2)}, u32[]{:S(2)}) async-start(bf16[3,2,128,256]{3,1,0,2:T(2,128)(2,1)} %copy.55), calls=%async_computation | async-start | bytes 786432 | tf_op jit(solution)/shard_map/all_to_all | solution.py:79
  184.2 0.4 copy.59
  184.6 7.6 %all-to-all-done = bf16[3,2,128,256]{3,1,0,2:T(2,128)(2,1)S(1)} async-done(((bf16[3,2,128,256]{3,1,0,2:T(2,128)(2,1)}), bf16[3,2,128,256]{3,1,0,2:T(2,128)(2,1)S(1)}, u32[]{:S(2)}, u32[]{:S(2)}) %all-to-all-start) | async-done | bytes 393248 | tf_op jit(solution)/shard_map/all_to_all | solution.py:79
  192.3 4.4 %stack.3 = bf16[8,3,2,128,256]{3,2,4,1,0:T(2,128)(2,1)} broadcast(bf16[3,2,128,256]{2,1,3,0:T(2,128)(2,1)S(1)} %copy.59), dimensions={1,2,3,4} | broadcast | bytes 3538944 | tf_op jit(solution)/shard_map/stack | solution.py:14
  196.6 5.2 %all-to-all-start.1 = ((bf16[8,3,2,128,256]{3,2,4,1,0:T(2,128)(2,1)}), bf16[8,3,2,128,256]{3,2,4,1,0:T(2,128)(2,1)}, u32[]{:S(2)}, u32[]{:S(2)}) async-start(bf16[8,3,2,128,256]{3,2,4,1,0:T(2,128)(2,1)} %stack.3), calls=%async_computation.1 | async-start | bytes 6291456 | tf_op jit(solution)/shard_map/all_to_all | solution.py:15
  202.6 0.1 fusion.46
  202.6 1.8 copy.69
  204.4 1.1 copy.70
  205.5 34.0 %all-to-all-done.1 = bf16[8,3,2,128,256]{3,2,4,1,0:T(2,128)(2,1)} async-done(((bf16[8,3,2,128,256]{3,2,4,1,0:T(2,128)(2,1)}), bf16[8,3,2,128,256]{3,2,4,1,0:T(2,128)(2,1)}, u32[]{:S(2)}, u32[]{:S(2)}) %all-to-all-start.1) | async-done | bytes 3145760 | tf_op jit(solution)/shard_map/all_to_all | solution.py:15
  239.5 4.2 %copy.60 = bf16[3,8,2,128,256]{3,2,1,4,0:T(2,128)(2,1)S(1)} copy(bf16[3,8,2,128,256]{3,2,4,0,1:T(2,128)(2,1)} %bitcast.11) | data formatting | bytes 6291456 | tf_op jit(solution)/shard_map/reshape | solution.py:15
  243.7 0.9 fusion
  244.6 2.6 fusion.4
  247.3 2.7 convolution_subtract_fusion
  249.9 3.5 %copy.68 = f32[3,128,16,128]{1,3,2,0:T(8,128)} copy(f32[3,128,16,128]{3,2,1,0:T(8,128)} %convolution_subtract_fusion) | data formatting | bytes 6291456 | tf_op jit(solution)/shard_map/reshape | solution.py:98
  253.5 5.0 %convolution_add_fusion = f32[3,128,16,128]{3,2,1,0:T(8,128)} fusion(f32[3,128,16,128]{3,2,1,0:T(8,128)} %fusion.4, bf16[3,16,16,128]{1,2,3,0:T(8,128)(2,1)S(1)} %copy.70, bf16[3,16,128,256]{2,1,3,0:T(8,128)(2,1)} %bitcast.41), kind=kOutput, calls=%fused_computation.3 | convolution fusion | flops 25952256 | bytes 8060928 | tf_op jit(solution)/shard_map/qsif,qsjf->qfij/dot_general | solution.py:88
  258.5 3.5 %copy.67 = f32[3,128,16,128]{1,3,2,0:T(8,128)} copy(f32[3,128,16,128]{3,2,1,0:T(8,128)} %convolution_add_fusion) | data formatting | bytes 6291456 | tf_op jit(solution)/shard_map/reshape | solution.py:97
  262.0 5.0 %fusion.22 = f32[3,2048,128]{2,1,0:T(8,128)S(1)} fusion(f32[3,128,2048]{1,2,0:T(8,128)} %bitcast.43, s32[128]{0:T(128)S(1)} %get-tuple-element.16, s32[128]{0:T(128)S(1)} %get-tuple-element.15), kind=kOutput, calls=%fused_computation.43 | convolution fusion | flops 1208188928 | bytes 6292480 | tf_op jit(solution)/shard_map/lf,qfx->qlx/dot_general | solution.py:99
  267.0 4.7 %multiply_bitcast_fusion = f32[3,128,2048]{1,2,0:T(8,128)} fusion(f32[3,2048,128]{2,1,0:T(8,128)S(1)} %fusion.22, f32[3,128,2048]{1,2,0:T(8,128)S(1)} %bitcast.42, f32[3]{0:T(128)S(1)} %compare_select_fusion.3, s32[128]{0:T(128)S(1)} %get-tuple-element.16, s32[128]{0:T(128)S(1)} %get-tuple-element.15), kind=kOutput, calls=%fused_computation.1 | convolution fusion | flops 1209778176 | bytes 9438220 | tf_op jit(solution)/shard_map/lf,qfx->qlx/dot_general | solution.py:100
  271.7 3.5 %copy.64 = f32[3,128,2048]{2,1,0:T(8,128)} copy(f32[3,128,2048]{1,2,0:T(8,128)} %multiply_bitcast_fusion) | data formatting | bytes 6291456 | tf_op jit(solution)/shard_map/mul | solution.py:105
  (26 shorter events, 0.2 us)
Async XLA Ops:
  6.5 2.1 copy-start
  6.5 5.0 %copy-start.4 = (s32[3,2]{0,1:T(2,128)S(1)}, s32[3,2]{0,1:T(2,128)}, u32[]{:S(2)}) copy-start(s32[3,2]{0,1:T(2,128)} %param.6) | copy-start | bytes 76
  6.5 5.1 %copy-start.5 = (s32[64]{0:T(128)S(1)}, s32[64]{0:T(128)}, u32[]{:S(2)}) copy-start(s32[64]{0:T(128)} %param.5) | copy-start | bytes 772
  6.5 159.7 %all-gather.2.cloned.1.call-start = ((), (), s32[]{:S(2)}) async-start(), calls=%async_computation.2 | async-start | bytes 8519680 | tf_op jit(solution)/shard_map/all_gather | solution.py:73
  171.6 20.6 %all-to-all-start = ((bf16[3,2,128,256]{3,1,0,2:T(2,128)(2,1)}), bf16[3,2,128,256]{3,1,0,2:T(2,128)(2,1)S(1)}, u32[]{:S(2)}, u32[]{:S(2)}) async-start(bf16[3,2,128,256]{3,1,0,2:T(2,128)(2,1)} %copy.55), calls=%async_computation | async-start | bytes 786432 | tf_op jit(solution)/shard_map/all_to_all | solution.py:79
  196.6 42.9 %all-to-all-start.1 = ((bf16[8,3,2,128,256]{3,2,4,1,0:T(2,128)(2,1)}), bf16[8,3,2,128,256]{3,2,4,1,0:T(2,128)(2,1)}, u32[]{:S(2)}, u32[]{:S(2)}) async-start(bf16[8,3,2,128,256]{3,2,4,1,0:T(2,128)(2,1)} %stack.3), calls=%async_computation.1 | async-start | bytes 6291456 | tf_op jit(solution)/shard_map/all_to_all | solution.py:15
  239.5 4.2 %copy-start.2 = (bf16[3,16,16,128]{1,2,3,0:T(8,128)(2,1)S(1)}, bf16[3,16,16,128]{1,2,3,0:T(8,128)(2,1)}, u32[]{:S(2)}) copy-start(bf16[3,16,16,128]{1,2,3,0:T(8,128)(2,1)} %copy.69) | copy-start | bytes 589828
  243.7 3.6 %copy-start.1 = (bf16[3,8,2,128,256]{3,2,1,4,0:T(2,128)(2,1)}, bf16[3,8,2,128,256]{3,2,1,4,0:T(2,128)(2,1)S(1)}, u32[]{:S(2)}) copy-start(bf16[3,8,2,128,256]{3,2,1,4,0:T(2,128)(2,1)S(1)} %copy.60) | copy-start | bytes 9437188
  262.0 5.0 %copy-start.3 = (f32[3,128,16,128]{1,3,2,0:T(8,128)S(1)}, f32[3,128,16,128]{1,3,2,0:T(8,128)}, u32[]{:S(2)}) copy-start(f32[3,128,16,128]{1,3,2,0:T(8,128)} %copy.68) | copy-start | bytes 9437188
Sparse Core Ops, SparseCore 0:
  11.7 154.5 all-gather.1
